TPU v7x, 512 devices: a whole 4x4x16 slice. The times are simulated.
512 devices in a mesh: dp: 32 (over x, y, core), expert: 16 (over z).
Axes of the slice: x: 4, y: 4, z: 16, core: 2. Of those that a mesh axis runs over, the one named last changes fastest.
Arguments:
- tokens: bfloat16 [4096, 2048], P('dp', 'expert'), may hold values from -6 to 6
- cotangent: bfloat16 [4096, 2048], P('dp', 'expert'), may hold values from -6 to 6
- expert_ids: int32 [4096, 8], P('dp'), may hold values from 0 to 127, all different within a row; in each aligned block of 128 rows (0 to 127, 128 to 255, ...) at most 16 rows name the same one
- gate_weights: float32 [4096, 8], P('dp'), may hold values from 0.05 to 1
- w_gate: bfloat16 [512, 192, 2048], P(('dp', 'expert')), may hold values from -0.125 to 0.125
- w_up: bfloat16 [512, 192, 2048], P(('dp', 'expert')), may hold values from -0.125 to 0.125
- w_down: bfloat16 [512, 192, 2048], P(('dp', 'expert')), may hold values from -0.21875 to 0.21875
Outputs:
- layer_out: bfloat16 [4096, 2048], P('dp', 'expert')
- grad_tokens: bfloat16 [4096, 2048], P('dp', 'expert')
- grad_gates: float32 [4096, 8], P('dp')
- grad_w_gate: bfloat16 [512, 192, 2048], P(('dp', 'expert'))
- grad_w_up: bfloat16 [512, 192, 2048], P(('dp', 'expert'))
- grad_w_down: bfloat16 [512, 192, 2048], P(('dp', 'expert'))
Inputs may be any that keep to these rules, and one draw needn't show every extreme that they name: `expert_ids`: each row names 8 different experts. In each aligned block of 128 rows (the rows of one index of dp) no expert is named by more than 16 rows, and in some block an expert is named by exactly 16 rows.
All inputs are finite; a program needn't handle non-finite values.
Results may differ from a plain program's by a relative error of at most 0.0064.
Values may be sent and summed in bfloat16 or wider, within the bound.
No kernel may reach another device: no remote copies, remote signals or barrier semaphores. Data moves between devices by JAX's collectives and lax.ppermute only.
A program may use at most 64 MiB of HBM per device.

v0:
```python
import jax
import jax.numpy as jnp
from jax import lax
from jax.sharding import PartitionSpec as P

SHARDS = 4


def silu_parts(preact):
    sigmoid_of = jax.nn.sigmoid(preact)
    activated = preact * sigmoid_of
    derivative = sigmoid_of * (1.0 + preact * (1.0 - sigmoid_of))
    return (activated, derivative)


def contract_last(first_op, second_op):
    return lax.dot_general(
        first_op, second_op, (((1,), (1,)), ((), ())), preferred_element_type=jnp.float32
    )


def contract_first(first_op, second_op):
    return lax.dot_general(
        first_op, second_op, (((0,), (0,)), ((), ())), preferred_element_type=jnp.float32
    )


def expert_rows(rows_x, rows_do, gate_w, up_w, down_w):
    pre_gate = contract_last(rows_x, gate_w)
    pre_up = contract_last(rows_x, up_w)
    activated, derivative = silu_parts(pre_gate)
    hidden = (activated * pre_up).astype(jnp.bfloat16)
    part_out = jnp.dot(hidden, down_w, preferred_element_type=jnp.float32).astype(jnp.bfloat16)
    d_hidden = contract_last(rows_do, down_w)
    d_pre_gate = (d_hidden * pre_up * derivative).astype(jnp.bfloat16)
    d_pre_up = (d_hidden * activated).astype(jnp.bfloat16)
    part_grad = (
        jnp.dot(d_pre_gate, gate_w, preferred_element_type=jnp.float32)
        + jnp.dot(d_pre_up, up_w, preferred_element_type=jnp.float32)
    ).astype(jnp.bfloat16)
    gradients = (
        contract_first(d_pre_gate, rows_x),
        contract_first(d_pre_up, rows_x),
        contract_first(hidden, rows_do),
    )
    return (part_out, part_grad, gradients)


def per_device(tokens, cotangent, expert_ids, gate_weights, w_gate, w_up, w_down):
    both = lax.all_gather(jnp.stack([tokens, cotangent]), "expert", axis=2, tiled=True)
    full_x, full_dy = (both[0], both[1])
    dp_count = lax.axis_size("dp")
    column_count = lax.axis_size("expert")
    column = lax.axis_index("expert")
    tok_count, chosen = expert_ids.shape
    features = full_x.shape[1]
    experts_all = dp_count * column_count // SHARDS
    capacity = min(tok_count, max(2, 2 * tok_count * chosen // experts_all))
    per_row = column_count // SHARDS
    assigned = tok_count * chosen
    flat_ids = expert_ids.reshape(-1)
    flat_gates = gate_weights.reshape(-1)
    owned_here = flat_ids % per_row == column // SHARDS
    target_row = flat_ids // per_row
    onehot = (
        (target_row[:, None] == jnp.arange(dp_count, dtype=jnp.int32)[None, :])
        & owned_here[:, None]
    ).astype(jnp.int32)
    rank_of = jnp.sum((jnp.cumsum(onehot, axis=0) - 1) * onehot, axis=1)
    target = jnp.where(owned_here, target_row * capacity + rank_of, dp_count * capacity)
    slot_src = (
        jnp.full((dp_count * capacity,), assigned, jnp.int32)
        .at[target]
        .set(jnp.arange(assigned, dtype=jnp.int32), mode="drop")
    )
    filled = slot_src < assigned
    safe_index = jnp.where(filled, slot_src, 0)
    slot_token = safe_index // chosen
    slot_gate = jnp.where(filled, flat_gates[safe_index], 0.0)
    slot_dy = full_dy[slot_token].astype(jnp.float32)
    send_x = jnp.where(filled[:, None], full_x[slot_token], jnp.zeros((), full_x.dtype)).reshape(
        dp_count, capacity, features
    )
    send_do = (
        (slot_gate[:, None] * slot_dy).astype(jnp.bfloat16).reshape(dp_count, capacity, features)
    )
    weights = (w_gate[0], w_up[0], w_down[0])
    recv = lax.all_to_all(
        jnp.concatenate([send_x, send_do], axis=1), "dp", split_axis=0, concat_axis=0, tiled=True
    )
    rows_x = recv[:, :capacity].reshape(dp_count * capacity, features)
    rows_do = recv[:, capacity:].reshape(dp_count * capacity, features)
    part_out, part_grad, gradients = expert_rows(rows_x, rows_do, *weights)
    back = lax.all_to_all(
        jnp.concatenate(
            [
                part_out.reshape(dp_count, capacity, features),
                part_grad.reshape(dp_count, capacity, features),
            ],
            axis=1,
        ),
        "dp",
        split_axis=0,
        concat_axis=0,
        tiled=True,
    )
    out_float = back[:, :capacity].reshape(dp_count * capacity, features).astype(jnp.float32)
    grad_float = back[:, capacity:].reshape(dp_count * capacity, features).astype(jnp.float32)
    out_part = (
        jnp.zeros((tok_count, features), jnp.float32)
        .at[slot_token]
        .add(slot_gate[:, None] * out_float)
    )
    grad_part = jnp.zeros((tok_count, features), jnp.float32).at[slot_token].add(grad_float)
    gate_terms = jnp.sum(slot_dy * out_float, axis=1)
    gate_part = (
        jnp.zeros((assigned,), jnp.float32)
        .at[slot_src]
        .add(gate_terms, mode="drop")
        .reshape(tok_count, chosen)
    )
    summed = lax.psum_scatter(
        jnp.stack([out_part, grad_part]), "expert", scatter_dimension=2, tiled=True
    )
    grad_gates = lax.psum(gate_part, "expert")
    return (
        summed[0].astype(jnp.bfloat16),
        summed[1].astype(jnp.bfloat16),
        grad_gates,
        gradients[0].astype(jnp.bfloat16)[None],
        gradients[1].astype(jnp.bfloat16)[None],
        gradients[2].astype(jnp.bfloat16)[None],
    )


def solution(mesh):
    placed = (
        P("dp", "expert"),
        P("dp", "expert"),
        P("dp", None),
        P("dp", None),
        P(("dp", "expert"), None, None),
        P(("dp", "expert"), None, None),
        P(("dp", "expert"), None, None),
    )
    return jax.shard_map(
        per_device,
        mesh=mesh,
        in_specs=placed,
        out_specs=(
            P("dp", "expert"),
            P("dp", "expert"),
            P("dp", None),
            P(("dp", "expert"), None, None),
            P(("dp", "expert"), None, None),
            P(("dp", "expert"), None, None),
        ),
        check_vma=False,
    )
```

profile of v0, /device:TPU:2, one launch (start us, length us, event | category | flops | bytes accessed | tf_op | source)
XLA Modules:
  0.0 319.4 jit_solution(1115190527233137053)
XLA Ops:
  7.2 1.5 pad_maximum_fusion.3
  8.8 0.8 copy.13
  9.9 0.8 copy.18
  10.8 9.0 %reduce-window.6 = s32[32,8,128]{2,1,0:T(8,128)S(1)} reduce-window(s32[32,8,128]{2,1,0:T(8,128)S(1)} %fusion.25, s32[]{:T(128)} %constant.66.clone.1), window={size=1x1x128 pad=0_0x0_0x127_0}, to_apply=%region_0.1 | reduce-window | flops 4161536 | bytes 262148 | tf_op jit(solution)/shard_map/reduce-window
  20.4 4.3 %scatter_custom_fusion = s32[512]{0:T(512)S(1)} fusion(s32[1024]{0:T(1024)S(1)} %bitcast.94, s32[1024]{0:T(1024)S(1)} %iota.11, s32[]{:T(128)} %constant.65.clone.1), kind=kCustom, calls=%fused_computation.100 | custom fusion | bytes 2052 | tf_op jit(solution)/shard_map/scatter | solution.py:74
  24.8 2.3 gather_fusion
  27.3 60.1 %all-gather.2.cloned.1.call-done = bf16[2,128,2048]{2,1,0:T(8,128)(2,1)} async-done(((bf16[2,128,128]{2,1,0:T(8,128)(2,1)}), bf16[2,128,2048]{2,1,0:T(8,128)(2,1)}) %all-gather.2.cloned.1.call-update) | async-done | bytes 1048592 | tf_op jit(solution)/shard_map/all_gather | solution.py:50
  87.3 1.3 slice_bitcast_fusion.1
  88.6 3.3 %gather_fusion.2 = bf16[512,2048]{1,0:T(8,128)(2,1)} fusion(bf16[128,2048]{1,0:T(8,128)(2,1)S(1)} %get-tuple-element.19, s32[1024]{0:T(1024)S(1)} %pad_clamp_fusion), kind=kCustom, calls=%fused_computation.2 | custom fusion | bytes 4196352 | tf_op jit(solution)/shard_map/gather | solution.py:80
  92.0 3.3 %gather_fusion.1 = bf16[512,2048]{1,0:T(8,128)(2,1)} fusion(bf16[128,2048]{1,0:T(8,128)(2,1)S(1)} %get-tuple-element.18, s32[1024]{0:T(1024)S(1)} %pad_clamp_fusion), kind=kCustom, calls=%fused_computation.1 | custom fusion | bytes 4196352 | tf_op jit(solution)/shard_map/gather | solution.py:81
  95.3 1.9 broadcast_select_fusion
  98.5 55.4 %all_to_all.10 = bf16[32,32,2048]{2,1,0:T(8,128)(2,1)S(1)} all-to-all(bf16[32,32,2048]{2,1,0:T(8,128)(2,1)S(1)} %pad_maximum_fusion), channel_id=1, replica_groups=mesh['dp'=32,'expert'=16] {'dp'}, dimensions={0} | all-to-all | bytes 8388608 | tf_op jit(solution)/shard_map/all_to_all | solution.py:88
  155.0 0.9 fusion.7
  155.9 0.8 copy-done.7
  156.7 0.8 fusion.15
  157.6 1.0 multiply_convert_fusion.2
  158.6 0.7 convolution_convert_fusion
  159.3 0.8 fusion.13
  160.1 0.8 add_convert_fusion
  161.4 54.4 %all_to_all.11 = bf16[32,32,2048]{2,1,0:T(8,128)(2,1)S(1)} all-to-all(bf16[32,32,2048]{2,1,0:T(8,128)(2,1)S(1)} %pad_maximum_fusion.1), channel_id=1, replica_groups=mesh['dp'=32,'expert'=16] {'dp'}, dimensions={0} | all-to-all | bytes 8388608 | tf_op jit(solution)/shard_map/all_to_all | solution.py:94
  215.8 2.5 slice_convert_fusion
  218.4 2.3 bitcast_multiply_fusion
  220.7 9.4 %scatter_custom_fusion.1 = f32[128,2048]{1,0:T(8,128)} fusion(s32[512]{0:T(512)S(1)} %get-tuple-element.26, f32[512,2048]{1,0:T(8,128)} %bitcast_multiply_fusion, f32[]{:T(128)} %constant.64.clone.1), kind=kCustom, calls=%fused_computation.40 | custom fusion | flops 1048576 | bytes 1049088 | tf_op jit(solution)/shard_map/scatter-add | solution.py:112
  230.2 9.1 %scatter_custom_fusion.2 = f32[128,2048]{1,0:T(8,128)} fusion(s32[512]{0:T(512)S(1)} %get-tuple-element.26, bf16[512,2048]{1,0:T(8,128)(2,1)} %bitcast.82, f32[]{:T(128)} %constant.64.clone.1), kind=kCustom, calls=%fused_computation.13 | custom fusion | flops 2097152 | bytes 3145732 | tf_op jit(solution)/shard_map/scatter-add | solution.py:114
  239.3 3.1 pad_maximum_fusion.2
  242.4 3.2 %fusion.6 = bf16[1,192,2048]{2,1,0:T(8,128)(2,1)} fusion(bf16[512,192]{0,1:T(8,128)(2,1)S(1)} %get-tuple-element.20, bf16[512,2048]{1,0:T(8,128)(2,1)} %bitcast.85), kind=kOutput, calls=%fused_computation.23 | convolution fusion | flops 403046400 | bytes 3080192 | tf_op jit(solution)/shard_map/dot_general | solution.py:23
  245.6 1.5 fusion.4
  247.1 1.5 fusion.5
  249.3 3.5 %scatter_custom_fusion.3 = f32[1024]{0:T(1024)S(1)} fusion(s32[512]{0:T(512)S(1)} %get-tuple-element.25, f32[512]{0:T(512)S(1)} %reshape.295, f32[]{:T(128)} %constant.64.clone.1), kind=kCustom, calls=%fused_computation.94 | custom fusion | flops 512 | bytes 4100 | tf_op jit(solution)/shard_map/scatter-add | solution.py:119
  252.8 54.7 %psum.7 = f32[128,8]{1,0:T(8,128)S(1)} all-reduce(f32[128,8]{1,0:T(8,128)S(1)} %reshape.239), channel_id=1, replica_groups=mesh['dp'=32,'expert'=16] {'expert'}, use_global_device_ids=true, to_apply=%region_9.10 | all-reduce | flops 1024 | bytes 8192 | tf_op jit(solution)/shard_map/psum | solution.py:125
  308.2 2.8 reduce-scatter.2.cloned.1.call-done
  311.0 0.9 convert.7
  (55 shorter events, 6.4 us)
Async XLA Ops:
  7.2 150.4 %copy-start = (bf16[1,192,2048]{2,1,0:T(8,128)(2,1)S(1)}, bf16[1,192,2048]{2,1,0:T(8,128)(2,1)}, u32[]{:S(2)}) copy-start(bf16[1,192,2048]{2,1,0:T(8,128)(2,1)} %param.12) | copy-start | bytes 2359300
  7.2 80.2 %all-gather.2.cloned.1.call-start = ((), (), s32[]{:S(2)}) async-start(), calls=%async_computation.3 | async-start | bytes 1114112 | tf_op jit(solution)/shard_map/all_gather | solution.py:50
  8.7 302.3 %reduce-scatter.2.cloned.1.call-start = ((), (), s32[]{:S(2)}) async-start(), calls=%async_computation.4 | async-start | bytes 2228224 | tf_op jit(solution)/shard_map/reduce_scatter | solution.py:122
  95.2 2.2 copy-start.3
  153.8 1.1 copy-start.8
  154.4 1.4 copy-start.6
  154.4 3.1 copy-start.4
  155.0 1.7 copy-start.7
  215.8 2.6 copy-start.1
  242.4 3.2 %copy-start.5 = (bf16[32,16,2048]{2,1,0:T(8,128)(2,1)S(1)}, bf16[32,16,2048]{2,1,0:T(8,128)(2,1)}, u32[]{:S(2)}) copy-start(bf16[32,16,2048]{2,1,0:T(8,128)(2,1)} %copy-done.4) | copy-start | bytes 6291460
  245.6 2.9 copy-start.2
Sparse Core Ops, SparseCore 0:
  10.6 76.7 all-gather.1
  242.5 68.4 reduce-scatter.1
where the time goes:
time: 320 us; the launch traced here: 319 us
  blocking collectives  164 us (51%)
  waiting for transfers between devices  62.9 us (20%)
  other arithmetic  45.8 us (14%)
  local copies, waits for them, and re-layouts  20.7 us (6%)
  between operations  14.4 us (4%)
  matrix products  11.1 us (3%)
    all_gather x1, waiting for transfers between devices, per_device(): lax.all_gather(jnp.stack([tokens, cotangent]), 'expert', axis=2, tiled=True)  60.1 us
    all_to_all x1, blocking collectives, per_device(): lax.all_to_all(jnp.concatenate([send_x, send_do], axis=1), 'dp', split_ax...  55.4 us
    psum x1, blocking collectives, per_device(): grad_gates = lax.psum(gate_part, 'expert')  54.7 us
    all_to_all x1, blocking collectives, per_device(): lax.all_to_all(jnp.concatenate([part_out.reshape(dp_count, capacity, feat...  54.4 us
    another operation x3, other arithmetic  9.96 us
    scatter-add x1, other arithmetic, per_device(): out_part = jnp.zeros((tok_count, features), jnp.float32).at[slot_token].a...  9.44 us
    scatter-add x1, other arithmetic, per_device(): jnp.zeros((tok_count, features), jnp.float32).at[slot_token].add(grad_float)  9.14 us
  transfers between devices with their start and end apart: 2, of which 2 were waited for; matrix products, arithmetic and copies ran while one was open for 9% of the time, Pallas kernels for 0%

commit v1 on v0

--- a/solution.py
+++ b/solution.py
@@ -47,7 +47,9 @@
 
 
 def per_device(tokens, cotangent, expert_ids, gate_weights, w_gate, w_up, w_down):
-    both = lax.all_gather(jnp.stack([tokens, cotangent]), "expert", axis=2, tiled=True)
+    own = jnp.stack([tokens, cotangent])
+    sent = jnp.stack([own] * lax.axis_size("expert"))
+    both = jnp.concatenate(lax.all_to_all(sent, "expert", 0, 0), axis=2)
     full_x, full_dy = (both[0], both[1])
     dp_count = lax.axis_size("dp")
     column_count = lax.axis_size("expert")

time: 320 us -> 309 us (0.966)
  the two profiles are of different devices: /device:TPU:2 before, /device:TPU:8 now
where the time goes in v1:
time: 309 us; the launch traced here: 308 us
  blocking collectives  169 us (55%)
  other arithmetic  45.2 us (15%)
  waiting for transfers between devices  32.8 us (11%)
  local copies, waits for them, and re-layouts  20.3 us (7%)
  starting transfers between devices  15.2 us (5%)
  between operations  14.4 us (5%)
  matrix products  11.1 us (4%)
    psum x1, blocking collectives, per_device(): grad_gates = lax.psum(gate_part, 'expert')  58.1 us
    all_to_all x1, blocking collectives, per_device(): lax.all_to_all(jnp.concatenate([send_x, send_do], axis=1), 'dp', split_ax...  56.6 us
    all_to_all x1, blocking collectives, per_device(): lax.all_to_all(jnp.concatenate([part_out.reshape(dp_count, capacity, feat...  54.4 us
    all_to_all x1, waiting for transfers between devices, per_device(): both = jnp.concatenate(lax.all_to_all(sent, 'expert', 0, 0), axis=2)  32.8 us
    all_to_all x1, starting transfers between devices, per_device(): both = jnp.concatenate(lax.all_to_all(sent, 'expert', 0, 0), axis=2)  15.2 us
    another operation x3, other arithmetic  9.96 us
    scatter-add x1, other arithmetic, per_device(): out_part = jnp.zeros((tok_count, features), jnp.float32).at[slot_token].a...  9.44 us
    scatter-add x1, other arithmetic, per_device(): jnp.zeros((tok_count, features), jnp.float32).at[slot_token].add(grad_float)  9.14 us
  transfers between devices with their start and end apart: 2, of which 1 were waited for; matrix products, arithmetic and copies ran while one was open for 9% of the time, Pallas kernels for 0%

profile of v1, /device:TPU:8, one launch (start us, length us, event | category | flops | bytes accessed | tf_op | source)
XLA Modules:
  0.0 308.2 jit_solution(9042202176892552777)
XLA Ops:
  7.2 0.9 pad_maximum_fusion.3
  8.1 1.2 stack.17
  9.3 15.2 %all-to-all-start = ((bf16[16,2,128,128]{3,2,1,0:T(8,128)(2,1)}), bf16[16,2,128,128]{3,2,1,0:T(8,128)(2,1)S(1)}, u32[]{:S(2)}, u32[]{:S(2)}) async-start(bf16[16,2,128,128]{3,2,1,0:T(8,128)(2,1)} %stack.17), calls=%async_computation | async-start | bytes 2097152 | tf_op jit(solution)/shard_map/all_to_all | solution.py:52
  25.2 9.0 %reduce-window.6 = s32[32,8,128]{2,1,0:T(8,128)S(1)} reduce-window(s32[32,8,128]{2,1,0:T(8,128)S(1)} %fusion.25, s32[]{:T(128)} %constant.66.clone.1), window={size=1x1x128 pad=0_0x0_0x127_0}, to_apply=%region_0.1 | reduce-window | flops 4161536 | bytes 262148 | tf_op jit(solution)/shard_map/reduce-window
  34.8 4.3 %scatter_custom_fusion = s32[512]{0:T(512)S(1)} fusion(s32[1024]{0:T(1024)S(1)} %bitcast.106, s32[1024]{0:T(1024)S(1)} %iota.11, s32[]{:T(128)} %constant.65.clone.1), kind=kCustom, calls=%fused_computation.100 | custom fusion | bytes 2052 | tf_op jit(solution)/shard_map/scatter | solution.py:76
  39.2 2.3 gather_fusion
  41.7 32.8 %all-to-all-done = bf16[16,2,128,128]{3,2,1,0:T(8,128)(2,1)S(1)} async-done(((bf16[16,2,128,128]{3,2,1,0:T(8,128)(2,1)}), bf16[16,2,128,128]{3,2,1,0:T(8,128)(2,1)S(1)}, u32[]{:S(2)}, u32[]{:S(2)}) %all-to-all-start) | async-done | bytes 1048608 | tf_op jit(solution)/shard_map/all_to_all | solution.py:52
  75.6 3.3 %gather_fusion.2 = bf16[512,2048]{1,0:T(8,128)(2,1)} fusion(bf16[128,2048]{1,0:T(8,128)(2,1)S(1)} %bitcast.84, s32[1024]{0:T(1024)S(1)} %pad_clamp_fusion), kind=kCustom, calls=%fused_computation.2 | custom fusion | bytes 4196352 | tf_op jit(solution)/shard_map/gather | solution.py:82
  78.9 3.3 %gather_fusion.1 = bf16[512,2048]{1,0:T(8,128)(2,1)} fusion(bf16[128,2048]{1,0:T(8,128)(2,1)S(1)} %bitcast.83, s32[1024]{0:T(1024)S(1)} %pad_clamp_fusion), kind=kCustom, calls=%fused_computation.1 | custom fusion | bytes 4196352 | tf_op jit(solution)/shard_map/gather | solution.py:83
  82.2 1.9 broadcast_select_fusion
  85.4 56.6 %all_to_all.15 = bf16[32,32,2048]{2,1,0:T(8,128)(2,1)S(1)} all-to-all(bf16[32,32,2048]{2,1,0:T(8,128)(2,1)S(1)} %pad_maximum_fusion), channel_id=1, replica_groups=mesh['dp'=32,'expert'=16] {'dp'}, dimensions={0} | all-to-all | bytes 8388608 | tf_op jit(solution)/shard_map/all_to_all | solution.py:90
  143.1 0.9 fusion.7
  144.0 0.8 copy-done.7
  144.9 0.8 fusion.15
  145.7 1.0 multiply_convert_fusion.2
  146.7 0.7 convolution_convert_fusion
  147.5 0.8 fusion.13
  148.2 0.8 add_convert_fusion
  149.6 54.4 %all_to_all.16 = bf16[32,32,2048]{2,1,0:T(8,128)(2,1)S(1)} all-to-all(bf16[32,32,2048]{2,1,0:T(8,128)(2,1)S(1)} %pad_maximum_fusion.1), channel_id=1, replica_groups=mesh['dp'=32,'expert'=16] {'dp'}, dimensions={0} | all-to-all | bytes 8388608 | tf_op jit(solution)/shard_map/all_to_all | solution.py:96
  204.0 2.5 slice_convert_fusion
  206.6 2.3 bitcast_multiply_fusion
  208.9 9.4 %scatter_custom_fusion.1 = f32[128,2048]{1,0:T(8,128)} fusion(s32[512]{0:T(512)S(1)} %get-tuple-element.32, f32[512,2048]{1,0:T(8,128)} %bitcast_multiply_fusion, f32[]{:T(128)} %constant.64.clone.1), kind=kCustom, calls=%fused_computation.40 | custom fusion | flops 1048576 | bytes 1049088 | tf_op jit(solution)/shard_map/scatter-add | solution.py:114
  218.3 9.1 %scatter_custom_fusion.2 = f32[128,2048]{1,0:T(8,128)} fusion(s32[512]{0:T(512)S(1)} %get-tuple-element.32, bf16[512,2048]{1,0:T(8,128)(2,1)} %bitcast.91, f32[]{:T(128)} %constant.64.clone.1), kind=kCustom, calls=%fused_computation.13 | custom fusion | flops 2097152 | bytes 3145732 | tf_op jit(solution)/shard_map/scatter-add | solution.py:116
  227.5 3.1 %pad_maximum_fusion.2 = f32[2,128,2048]{2,1,0:T(8,128)} fusion(f32[1,128,2048]{2,1,0:T(8,128)} %bitcast.98, f32[1,128,2048]{2,1,0:T(8,128)} %bitcast.97), kind=kLoop, calls=%fused_computation.25 | loop fusion | flops 524288 | bytes 4194304 | tf_op jit(solution)/shard_map/stack | solution.py:125
  230.6 3.2 %fusion.6 = bf16[1,192,2048]{2,1,0:T(8,128)(2,1)} fusion(bf16[512,192]{0,1:T(8,128)(2,1)S(1)} %get-tuple-element.26, bf16[512,2048]{1,0:T(8,128)(2,1)} %bitcast.94), kind=kOutput, calls=%fused_computation.23 | convolution fusion | flops 403046400 | bytes 3080192 | tf_op jit(solution)/shard_map/dot_general | solution.py:23
  233.8 1.5 fusion.4
  235.3 1.5 fusion.5
  236.7 0.6 fusion.1
  237.4 3.5 %scatter_custom_fusion.3 = f32[1024]{0:T(1024)S(1)} fusion(s32[512]{0:T(512)S(1)} %get-tuple-element.31, f32[512]{0:T(512)S(1)} %reshape.306, f32[]{:T(128)} %constant.64.clone.1), kind=kCustom, calls=%fused_computation.94 | custom fusion | flops 512 | bytes 4100 | tf_op jit(solution)/shard_map/scatter-add | solution.py:121
  241.0 58.1 %psum.7 = f32[128,8]{1,0:T(8,128)S(1)} all-reduce(f32[128,8]{1,0:T(8,128)S(1)} %reshape.250), channel_id=1, replica_groups=mesh['dp'=32,'expert'=16] {'expert'}, use_global_device_ids=true, to_apply=%region_9.10 | all-reduce | flops 1024 | bytes 8192 | tf_op jit(solution)/shard_map/psum | solution.py:127
  299.1 0.7 copy.28
  299.8 0.9 convert.7
  (63 shorter events, 6.3 us)
Async XLA Ops:
  7.2 138.6 %copy-start = (bf16[1,192,2048]{2,1,0:T(8,128)(2,1)S(1)}, bf16[1,192,2048]{2,1,0:T(8,128)(2,1)}, u32[]{:S(2)}) copy-start(bf16[1,192,2048]{2,1,0:T(8,128)(2,1)} %param.12) | copy-start | bytes 2359300
  7.2 17.4 %copy-start.9 = (s32[128,8]{0,1:T(8,128)S(1)}, s32[128,8]{0,1:T(8,128)}, u32[]{:S(2)}) copy-start(s32[128,8]{0,1:T(8,128)} %param.9) | copy-start | bytes 12292
  7.2 17.7 %copy-start.10 = (f32[128,8]{0,1:T(8,128)S(1)}, f32[128,8]{0,1:T(8,128)}, u32[]{:S(2)}) copy-start(f32[128,8]{0,1:T(8,128)} %param.10) | copy-start | bytes 12292
  9.3 65.2 %all-to-all-start = ((bf16[16,2,128,128]{3,2,1,0:T(8,128)(2,1)}), bf16[16,2,128,128]{3,2,1,0:T(8,128)(2,1)S(1)}, u32[]{:S(2)}, u32[]{:S(2)}) async-start(bf16[16,2,128,128]{3,2,1,0:T(8,128)(2,1)} %stack.17), calls=%async_computation | async-start | bytes 2097152 | tf_op jit(solution)/shard_map/all_to_all | solution.py:52
  24.5 275.3 %reduce-scatter.2.cloned.1.call-start = ((), (), s32[]{:S(2)}) async-start(), calls=%async_computation.4 | async-start | bytes 2228224 | tf_op jit(solution)/shard_map/reduce_scatter | solution.py:124
  82.2 2.2 copy-start.3
  142.0 1.1 copy-start.8
  142.6 1.4 copy-start.6
  142.6 3.1 %copy-start.4 = (bf16[32,16,2048]{2,1,0:T(8,128)(2,1)}, bf16[32,16,2048]{2,1,0:T(8,128)(2,1)S(1)}, u32[]{:S(2)}) copy-start(bf16[32,16,2048]{2,1,0:T(8,128)(2,1)S(1)} %get-tuple-element.23) | copy-start | bytes 6291460
  143.1 1.7 copy-start.7
  204.0 2.6 copy-start.1
  230.6 3.2 %copy-start.5 = (bf16[32,16,2048]{2,1,0:T(8,128)(2,1)S(1)}, bf16[32,16,2048]{2,1,0:T(8,128)(2,1)}, u32[]{:S(2)}) copy-start(bf16[32,16,2048]{2,1,0:T(8,128)(2,1)} %copy-done.4) | copy-start | bytes 6291460
  233.8 2.9 copy-start.2
Sparse Core Ops, SparseCore 0:
  230.7 68.2 reduce-scatter.1
